TPU v7x, 512 devices: a whole 4x4x16 slice. The times are simulated.
512 devices in a mesh: dp: 8 (over y, core), ctx: 64 (over z, x).
Axes of the slice: x: 4, y: 4, z: 16, core: 2. Of those that a mesh axis runs over, the one named last changes fastest.
Arguments:
- query_in: bfloat16 [8, 8192, 1792], P('dp', 'ctx'), may hold values from -8 to 8
- key_in: bfloat16 [8, 8192, 256], P('dp', 'ctx'), may hold values from -4 to 4
- value_input: bfloat16 [8, 8192, 256], P('dp', 'ctx'), may hold values from -4 to 4
- output_gradient: bfloat16 [8, 8192, 1792], P('dp', 'ctx'), may hold values from -5 to 5
- doc_ids: int32 [8, 8192], P('dp', 'ctx'), may hold values from 0 to 1, as said below
- query_bias: float32 [1792], replicated, may hold values from -2 to 2
Outputs:
- attended: bfloat16 [8, 8192, 1792], P('dp', 'ctx')
- grad_query: bfloat16 [8, 8192, 1792], P('dp', 'ctx')
- key_gradient: bfloat16 [8, 8192, 256], P('dp', 'ctx')
- value_gradient: bfloat16 [8, 8192, 256], P('dp', 'ctx')
- grad_bias: float32 [1792], replicated
Inputs may be any that keep to these rules, and one draw needn't show every extreme that they name: `doc_ids`: ids never fall along a sequence; each of the 2 documents of a sequence holds 2048 to 6144 tokens, and together they fill all 8192 tokens.
All inputs are finite; a program needn't handle non-finite values.
Results may differ from a plain program's by a relative error of at most 0.019.
Values may be sent and summed in bfloat16 or wider, within the bound.
A program may use at most 64 MiB of HBM per device.

v0:
```python
import math
import jax
import jax.numpy as jnp
from jax import lax
from jax.sharding import PartitionSpec as P

QUERY_HEADS = 14
KEY_VALUE_HEADS = 2
HEAD_SIZE = 128
GROUP_SIZE = 7
BLK = 128
WB = 16


def passed_along(value, axis, steps):
    count = lax.axis_size(axis)
    first, last = (max(0, -steps), min(count, count - steps))
    return lax.ppermute(value, axis, [(source, source + steps) for source in range(first, last)])


def split_pack(packed_block):
    head_size_width = KEY_VALUE_HEADS * HEAD_SIZE
    key_head_rows = packed_block[:, :head_size_width].reshape(
        packed_block.shape[0], KEY_VALUE_HEADS, HEAD_SIZE
    )
    value_head_rows = packed_block[:, head_size_width:].reshape(
        packed_block.shape[0], KEY_VALUE_HEADS, HEAD_SIZE
    )
    return (key_head_rows, value_head_rows)


def local(query_in, key_in, value_input, output_gradient, doc_ids, query_bias):
    sharded_rows = query_in.shape[1]
    ctx_count = lax.axis_size("ctx")
    ctx_rank = lax.axis_index("ctx")
    score_scale = 1.0 / math.sqrt(HEAD_SIZE)
    blocks_here = sharded_rows // BLK
    window_slots = min((WB - 1 + blocks_here - 1) // blocks_here, ctx_count - 1) + 1
    group_slots = max(1, min(window_slots, 512 // sharded_rows))
    group_count = -(-window_slots // group_slots)
    padded_slots = group_count * group_slots
    grouped_rows = group_slots * sharded_rows
    packed_width = 2 * KEY_VALUE_HEADS * HEAD_SIZE
    query_rows = (query_in[0].astype(jnp.float32) + query_bias).astype(jnp.bfloat16)
    query_head_rows = query_rows.reshape(sharded_rows, KEY_VALUE_HEADS, GROUP_SIZE, HEAD_SIZE)
    gradient_heads = output_gradient[0].reshape(
        sharded_rows, KEY_VALUE_HEADS, GROUP_SIZE, HEAD_SIZE
    )
    own_pack = jnp.concatenate([key_in[0], value_input[0]], axis=1)
    own_docs = doc_ids[0]
    query_pos = ctx_rank * sharded_rows + jnp.arange(sharded_rows, dtype=jnp.int32)
    first_pack = jnp.concatenate(
        [own_pack[None], jnp.zeros((window_slots - 1, sharded_rows, packed_width), jnp.bfloat16)],
        axis=0,
    )
    first_docs = jnp.concatenate(
        [own_docs[None], jnp.zeros((window_slots - 1, sharded_rows), jnp.int32)], axis=0
    )

    def pass_on(step_index, running):
        stored_pack, stored_docs, moving_pack, moving_docs = running
        moving_pack, moving_docs = passed_along((moving_pack, moving_docs), "ctx", 1)
        stored_pack = lax.dynamic_update_index_in_dim(stored_pack, moving_pack, step_index, 0)
        stored_docs = lax.dynamic_update_index_in_dim(stored_docs, moving_docs, step_index, 0)
        return (stored_pack, stored_docs, moving_pack, moving_docs)

    window_pack, window_docs, _, _ = lax.fori_loop(
        1, window_slots, pass_on, (first_pack, first_docs, own_pack, own_docs)
    )
    spare_slots = padded_slots - window_slots
    window_pack = jnp.concatenate(
        [window_pack, jnp.zeros((spare_slots, sharded_rows, packed_width), jnp.bfloat16)], axis=0
    )
    window_pack = window_pack.reshape(group_count, grouped_rows, packed_width)
    window_docs = jnp.concatenate(
        [window_docs, jnp.zeros((spare_slots, sharded_rows), jnp.int32)], axis=0
    )
    window_docs = window_docs.reshape(group_count, grouped_rows)
    group_ids = jnp.arange(group_count, dtype=jnp.int32)

    def group_mask(group_index, docs_block):
        key_index = jnp.arange(grouped_rows, dtype=jnp.int32)
        slot_index = group_index * group_slots + key_index // sharded_rows
        key_pos = (ctx_rank - slot_index) * sharded_rows + key_index % sharded_rows
        inside = ((slot_index < window_slots) & (key_pos >= 0))[None, :]
        causal = key_pos[None, :] <= query_pos[:, None]
        near = query_pos[:, None] // BLK - key_pos[None, :] // BLK < WB
        same_doc = own_docs[:, None] == docs_block[None, :]
        return inside & causal & near & same_doc

    def group_scores(packed_block, allowed):
        key_head_rows, value_head_rows = split_pack(packed_block)
        scores = (
            jnp.einsum(
                "qgnd,kgd->gnqk", query_head_rows, key_head_rows, preferred_element_type=jnp.float32
            )
            * score_scale
        )
        return (jnp.where(allowed[None, None], scores, -jnp.inf), key_head_rows, value_head_rows)

    def forward_work(running, packed_block, allowed):
        row_max, row_sum, weighted = running
        scores, key_head_rows, value_head_rows = group_scores(packed_block, allowed)
        new_max = jnp.maximum(row_max, jnp.max(scores, axis=-1))
        rescale = jnp.exp(row_max - new_max)
        weights = jnp.exp(scores - new_max[..., None])
        row_sum = row_sum * rescale + jnp.sum(weights, axis=-1)
        weighted = weighted * rescale[..., None] + jnp.einsum(
            "gnqk,kgd->gnqd", weights, value_head_rows.astype(jnp.float32)
        )
        return (new_max, row_sum, weighted)

    def forward_step(running, inputs):
        packed_block, docs_block, group_index = inputs
        allowed = group_mask(group_index, docs_block)
        running = forward_work(running, packed_block, allowed)
        return (running, None)

    statistics_shape = (KEY_VALUE_HEADS, GROUP_SIZE, sharded_rows)
    start_stats = (
        jnp.full(statistics_shape, -jnp.inf, jnp.float32),
        jnp.zeros(statistics_shape, jnp.float32),
        jnp.zeros(statistics_shape + (HEAD_SIZE,), jnp.float32),
    )
    (row_max, row_sum, weighted), _ = lax.scan(
        forward_step, start_stats, (window_pack, window_docs, group_ids)
    )
    log_total = row_max + jnp.log(row_sum)
    attended = jnp.transpose(weighted / row_sum[..., None], (2, 0, 1, 3)).astype(jnp.bfloat16)
    row_dot = jnp.einsum(
        "qgnd,qgnd->gnq", gradient_heads, attended, preferred_element_type=jnp.float32
    )

    def backward_work(grad_query, packed_block, allowed):
        scores, key_head_rows, value_head_rows = group_scores(packed_block, allowed)
        attend = jnp.exp(scores - log_total[..., None])
        grad_prob = jnp.einsum(
            "qgnd,kgd->gnqk", gradient_heads, value_head_rows, preferred_element_type=jnp.float32
        )
        grad_score = (attend * (grad_prob - row_dot[..., None])).astype(jnp.bfloat16)
        grad_query = grad_query + jnp.einsum(
            "gnqk,kgd->qgnd", grad_score, key_head_rows, preferred_element_type=jnp.float32
        )
        key_gradient = (
            jnp.einsum(
                "gnqk,qgnd->kgd", grad_score, query_head_rows, preferred_element_type=jnp.float32
            )
            * score_scale
        )
        value_gradient = jnp.einsum(
            "gnqk,qgnd->kgd",
            attend.astype(jnp.bfloat16),
            gradient_heads,
            preferred_element_type=jnp.float32,
        )
        partial_value = jnp.concatenate(
            [
                key_gradient.reshape(grouped_rows, KEY_VALUE_HEADS * HEAD_SIZE),
                value_gradient.reshape(grouped_rows, KEY_VALUE_HEADS * HEAD_SIZE),
            ],
            axis=1,
        )
        return (grad_query, partial_value)

    def backward_step(grad_query, inputs):
        packed_block, docs_block, group_index = inputs
        allowed = group_mask(group_index, docs_block)
        return backward_work(grad_query, packed_block, allowed)

    grad_query, partials = lax.scan(
        backward_step,
        jnp.zeros((sharded_rows, KEY_VALUE_HEADS, GROUP_SIZE, HEAD_SIZE), jnp.float32),
        (window_pack, window_docs, group_ids),
    )
    partials = partials.reshape(padded_slots, sharded_rows, packed_width)
    query_grad = (grad_query * score_scale).reshape(sharded_rows, QUERY_HEADS * HEAD_SIZE)

    def return_partial(step_index, running):
        returned = passed_along(running, "ctx", -1)
        return returned + lax.dynamic_index_in_dim(
            partials, window_slots - 1 - step_index, 0, keepdims=False
        )

    summed_total = lax.fori_loop(1, window_slots, return_partial, partials[window_slots - 1])
    key_gradient = summed_total[:, : KEY_VALUE_HEADS * HEAD_SIZE].astype(jnp.bfloat16)
    value_gradient = summed_total[:, KEY_VALUE_HEADS * HEAD_SIZE :].astype(jnp.bfloat16)
    grad_bias = lax.psum(jnp.sum(query_grad, axis=0), ("dp", "ctx"))
    attended_out = attended.reshape(sharded_rows, QUERY_HEADS * HEAD_SIZE)
    return (
        attended_out[None],
        query_grad.astype(jnp.bfloat16)[None],
        key_gradient[None],
        value_gradient[None],
        grad_bias,
    )


def solution(mesh):
    placed = (
        P("dp", "ctx", None),
        P("dp", "ctx", None),
        P("dp", "ctx", None),
        P("dp", "ctx", None),
        P("dp", "ctx"),
        P(),
    )
    return jax.shard_map(
        local,
        mesh=mesh,
        in_specs=placed,
        out_specs=(
            P("dp", "ctx", None),
            P("dp", "ctx", None),
            P("dp", "ctx", None),
            P("dp", "ctx", None),
            P(),
        ),
        check_vma=False,
    )
```

profile of v0, /device:TPU:1, one launch (start us, length us, event | category | flops | bytes accessed | tf_op | source)
XLA Modules:
  0.0 563.7 jit_solution(16847469983181574787)
XLA Ops:
  8.9 138.4 %while.72 = (s32[]{:T(128)}, bf16[16,128,512]{2,1,0:T(8,128)(2,1)}, s32[16,128]{1,0:T(8,128)S(1)}, bf16[128,512]{1,0:T(8,128)(2,1)S(1)}, s32[128]{0:T(128)S(1)}, /*index=5*/s32[]{:T(128)}, s32[]{:T(128)}, s32[]{:T(128)}) while((s32[]{:T(128)}, bf16[16,128,512]{2,1,0:T(8,128)(2,1)}, s32[16,128]{1,0:T(8,128)S(1)}, ...), condition=%wide.region_1.2_spmd, body=%wide.region_0.1_spmd.sunk | while | flops 5 | bytes 1052879 | solution.py:67
  29.2 4.8 collective-permute-start.1
  102.5 4.8 collective-permute-start.1
  131.0 4.5 collective-permute-start.1
  140.5 5.3 collective-permute-start.1
  151.5 23.1 %while.74 = (s32[]{:T(128)}, f32[2,7,128]{2,1,0:T(8,128)S(1)}, f32[2,7,128]{2,1,0:T(8,128)S(1)}, f32[2,7,128,128]{3,2,1,0:T(8,128)S(1)}, s32[4]{0:T(128)S(1)}, /...) while((s32[]{:T(128)}, f32[2,7,128]{2,1,0:T(8,128)S(1)}, ...), condition=%wide.region_5.6_spmd.clone.clone.clone, body=%wide.region_2.5_spmd.clone.clone.clone.sunk | while | flops 480120704 | bytes 16320205 | solution.py:125
  179.3 42.8 %while.75 = (s32[]{:T(128)}, f32[128,2,7,128]{0,3,2,1:T(8,128)S(1)}, f32[4,512,512]{2,1,0:T(8,128)}, bf16[4,512,512]{1,2,0:T(8,128)(2,1)}, s32[4]{0:T(128)S(1)},...) while((s32[]{:T(128)}, ...), condition=%wide.region_7.8_spmd.clone.clone.clone, body=%wide.region_6.7_spmd.clone.clone.clone.sunk | while | flops 1184918656 | bytes 30644960 | solution.py:170
  223.1 163.2 %while.73 = (s32[]{:T(128)}, f32[128,512]{1,0:T(8,128)S(1)}, f32[16,128,512]{2,1,0:T(8,128)}, s32[]{:T(128)}, s32[]{:T(128)}, /*index=5*/s32[]{:T(128)}, s32[]{:T(128)}) while((s32[]{:T(128)}, f32[128,512]{1,0:T(8,128)S(1)}, f32[16,128,512]{2,1,0:T(8,128)}, s32[]{:T(128)}, s32[]{:T(128)}, /*index=5*/s32[]{:T(128)}, s32[]{:T(128)}) %tuple.177), condition=%wide.region_9.10_spmd, body=%wide.region_8.9_spmd.sunk | while | flops 65542 | bytes 1835175 | solution.py:184
  224.4 6.0 %collective-permute-done.2 = f32[128,512]{1,0:T(8,128)S(1)} collective-permute-done((f32[128,512]{1,0:T(8,128)S(1)}, f32[128,512]{1,0:T(8,128)S(1)}, u32[]{:S(2)}, u32[]{:S(2)}) %collective-permute-start.2) | collective-permute-done | bytes 262176 | tf_op jit(solution)/shard_map/while/body/eval_jaxpr/ppermute | solution.py:18
  232.7 7.8 %collective-permute-done.2 = f32[128,512]{1,0:T(8,128)S(1)} collective-permute-done((f32[128,512]{1,0:T(8,128)S(1)}, f32[128,512]{1,0:T(8,128)S(1)}, u32[]{:S(2)}, u32[]{:S(2)}) %collective-permute-start.2) | collective-permute-done | bytes 262176 | tf_op jit(solution)/shard_map/while/body/eval_jaxpr/ppermute | solution.py:18
  242.8 7.7 %collective-permute-done.2 = f32[128,512]{1,0:T(8,128)S(1)} collective-permute-done((f32[128,512]{1,0:T(8,128)S(1)}, f32[128,512]{1,0:T(8,128)S(1)}, u32[]{:S(2)}, u32[]{:S(2)}) %collective-permute-start.2) | collective-permute-done | bytes 262176 | tf_op jit(solution)/shard_map/while/body/eval_jaxpr/ppermute | solution.py:18
  252.8 10.2 %collective-permute-done.2 = f32[128,512]{1,0:T(8,128)S(1)} collective-permute-done((f32[128,512]{1,0:T(8,128)S(1)}, f32[128,512]{1,0:T(8,128)S(1)}, u32[]{:S(2)}, u32[]{:S(2)}) %collective-permute-start.2) | collective-permute-done | bytes 262176 | tf_op jit(solution)/shard_map/while/body/eval_jaxpr/ppermute | solution.py:18
  265.3 11.4 %collective-permute-done.2 = f32[128,512]{1,0:T(8,128)S(1)} collective-permute-done((f32[128,512]{1,0:T(8,128)S(1)}, f32[128,512]{1,0:T(8,128)S(1)}, u32[]{:S(2)}, u32[]{:S(2)}) %collective-permute-start.2) | collective-permute-done | bytes 262176 | tf_op jit(solution)/shard_map/while/body/eval_jaxpr/ppermute | solution.py:18
  279.0 9.2 %collective-permute-done.2 = f32[128,512]{1,0:T(8,128)S(1)} collective-permute-done((f32[128,512]{1,0:T(8,128)S(1)}, f32[128,512]{1,0:T(8,128)S(1)}, u32[]{:S(2)}, u32[]{:S(2)}) %collective-permute-start.2) | collective-permute-done | bytes 262176 | tf_op jit(solution)/shard_map/while/body/eval_jaxpr/ppermute | solution.py:18
  290.5 7.4 %collective-permute-done.2 = f32[128,512]{1,0:T(8,128)S(1)} collective-permute-done((f32[128,512]{1,0:T(8,128)S(1)}, f32[128,512]{1,0:T(8,128)S(1)}, u32[]{:S(2)}, u32[]{:S(2)}) %collective-permute-start.2) | collective-permute-done | bytes 262176 | tf_op jit(solution)/shard_map/while/body/eval_jaxpr/ppermute | solution.py:18
  300.1 6.8 %collective-permute-done.2 = f32[128,512]{1,0:T(8,128)S(1)} collective-permute-done((f32[128,512]{1,0:T(8,128)S(1)}, f32[128,512]{1,0:T(8,128)S(1)}, u32[]{:S(2)}, u32[]{:S(2)}) %collective-permute-start.2) | collective-permute-done | bytes 262176 | tf_op jit(solution)/shard_map/while/body/eval_jaxpr/ppermute | solution.py:18
  309.3 7.6 %collective-permute-done.2 = f32[128,512]{1,0:T(8,128)S(1)} collective-permute-done((f32[128,512]{1,0:T(8,128)S(1)}, f32[128,512]{1,0:T(8,128)S(1)}, u32[]{:S(2)}, u32[]{:S(2)}) %collective-permute-start.2) | collective-permute-done | bytes 262176 | tf_op jit(solution)/shard_map/while/body/eval_jaxpr/ppermute | solution.py:18
  319.2 7.9 %collective-permute-done.2 = f32[128,512]{1,0:T(8,128)S(1)} collective-permute-done((f32[128,512]{1,0:T(8,128)S(1)}, f32[128,512]{1,0:T(8,128)S(1)}, u32[]{:S(2)}, u32[]{:S(2)}) %collective-permute-start.2) | collective-permute-done | bytes 262176 | tf_op jit(solution)/shard_map/while/body/eval_jaxpr/ppermute | solution.py:18
  329.4 7.9 %collective-permute-done.2 = f32[128,512]{1,0:T(8,128)S(1)} collective-permute-done((f32[128,512]{1,0:T(8,128)S(1)}, f32[128,512]{1,0:T(8,128)S(1)}, u32[]{:S(2)}, u32[]{:S(2)}) %collective-permute-start.2) | collective-permute-done | bytes 262176 | tf_op jit(solution)/shard_map/while/body/eval_jaxpr/ppermute | solution.py:18
  339.7 7.9 %collective-permute-done.2 = f32[128,512]{1,0:T(8,128)S(1)} collective-permute-done((f32[128,512]{1,0:T(8,128)S(1)}, f32[128,512]{1,0:T(8,128)S(1)}, u32[]{:S(2)}, u32[]{:S(2)}) %collective-permute-start.2) | collective-permute-done | bytes 262176 | tf_op jit(solution)/shard_map/while/body/eval_jaxpr/ppermute | solution.py:18
  349.9 8.8 %collective-permute-done.2 = f32[128,512]{1,0:T(8,128)S(1)} collective-permute-done((f32[128,512]{1,0:T(8,128)S(1)}, f32[128,512]{1,0:T(8,128)S(1)}, u32[]{:S(2)}, u32[]{:S(2)}) %collective-permute-start.2) | collective-permute-done | bytes 262176 | tf_op jit(solution)/shard_map/while/body/eval_jaxpr/ppermute | solution.py:18
  361.0 10.4 %collective-permute-done.2 = f32[128,512]{1,0:T(8,128)S(1)} collective-permute-done((f32[128,512]{1,0:T(8,128)S(1)}, f32[128,512]{1,0:T(8,128)S(1)}, u32[]{:S(2)}, u32[]{:S(2)}) %collective-permute-start.2) | collective-permute-done | bytes 262176 | tf_op jit(solution)/shard_map/while/body/eval_jaxpr/ppermute | solution.py:18
  373.7 11.5 %collective-permute-done.2 = f32[128,512]{1,0:T(8,128)S(1)} collective-permute-done((f32[128,512]{1,0:T(8,128)S(1)}, f32[128,512]{1,0:T(8,128)S(1)}, u32[]{:S(2)}, u32[]{:S(2)}) %collective-permute-start.2) | collective-permute-done | bytes 262176 | tf_op jit(solution)/shard_map/while/body/eval_jaxpr/ppermute | solution.py:18
  387.3 175.4 %psum.7 = f32[1792]{0:T(1024)} all-reduce(f32[1792]{0:T(1024)S(1)} %reduce_sum.25), channel_id=1, replica_groups=mesh['dp'=8,'ctx'=64] {'dp','ctx'}, use_global_device_ids=true, to_apply=%region_11.12 | all-reduce | flops 1792 | bytes 14336 | tf_op jit(solution)/shard_map/psum | solution.py:187
  (298 shorter events, 232.6 us)
Async XLA Ops:
  25.7 9.1 %collective-permute-start = (bf16[128,512]{1,0:T(8,128)(2,1)S(1)}, bf16[128,512]{1,0:T(8,128)(2,1)S(1)}, u32[]{:S(2)}, u32[]{:S(2)}) collective-permute-start(bf16[128,512]{1,0:T(8,128)(2,1)S(1)} %get-tuple-element.1222), channel_id=1, source_target_pairs={{0,1},{1,2},{2,3},{3,4},{4,5},{5,6},{6,7},{7,8},{8,9},{9,10},{10,1... | collective-permute-start | bytes 393224 | tf_op jit(solution)/shard_map/while/body/eval_jaxpr/ppermute | solution.py:18
  35.5 8.3 %collective-permute-start = (bf16[128,512]{1,0:T(8,128)(2,1)S(1)}, bf16[128,512]{1,0:T(8,128)(2,1)S(1)}, u32[]{:S(2)}, u32[]{:S(2)}) collective-permute-start(bf16[128,512]{1,0:T(8,128)(2,1)S(1)} %get-tuple-element.1222), channel_id=1, source_target_pairs={{0,1},{1,2},{2,3},{3,4},{4,5},{5,6},{6,7},{7,8},{8,9},{9,10},{10,1... | collective-permute-start | bytes 393224 | tf_op jit(solution)/shard_map/while/body/eval_jaxpr/ppermute | solution.py:18
  44.5 8.3 %collective-permute-start = (bf16[128,512]{1,0:T(8,128)(2,1)S(1)}, bf16[128,512]{1,0:T(8,128)(2,1)S(1)}, u32[]{:S(2)}, u32[]{:S(2)}) collective-permute-start(bf16[128,512]{1,0:T(8,128)(2,1)S(1)} %get-tuple-element.1222), channel_id=1, source_target_pairs={{0,1},{1,2},{2,3},{3,4},{4,5},{5,6},{6,7},{7,8},{8,9},{9,10},{10,1... | collective-permute-start | bytes 393224 | tf_op jit(solution)/shard_map/while/body/eval_jaxpr/ppermute | solution.py:18
  53.5 8.3 %collective-permute-start = (bf16[128,512]{1,0:T(8,128)(2,1)S(1)}, bf16[128,512]{1,0:T(8,128)(2,1)S(1)}, u32[]{:S(2)}, u32[]{:S(2)}) collective-permute-start(bf16[128,512]{1,0:T(8,128)(2,1)S(1)} %get-tuple-element.1222), channel_id=1, source_target_pairs={{0,1},{1,2},{2,3},{3,4},{4,5},{5,6},{6,7},{7,8},{8,9},{9,10},{10,1... | collective-permute-start | bytes 393224 | tf_op jit(solution)/shard_map/while/body/eval_jaxpr/ppermute | solution.py:18
  62.6 8.3 %collective-permute-start = (bf16[128,512]{1,0:T(8,128)(2,1)S(1)}, bf16[128,512]{1,0:T(8,128)(2,1)S(1)}, u32[]{:S(2)}, u32[]{:S(2)}) collective-permute-start(bf16[128,512]{1,0:T(8,128)(2,1)S(1)} %get-tuple-element.1222), channel_id=1, source_target_pairs={{0,1},{1,2},{2,3},{3,4},{4,5},{5,6},{6,7},{7,8},{8,9},{9,10},{10,1... | collective-permute-start | bytes 393224 | tf_op jit(solution)/shard_map/while/body/eval_jaxpr/ppermute | solution.py:18
  80.6 8.4 %collective-permute-start = (bf16[128,512]{1,0:T(8,128)(2,1)S(1)}, bf16[128,512]{1,0:T(8,128)(2,1)S(1)}, u32[]{:S(2)}, u32[]{:S(2)}) collective-permute-start(bf16[128,512]{1,0:T(8,128)(2,1)S(1)} %get-tuple-element.1222), channel_id=1, source_target_pairs={{0,1},{1,2},{2,3},{3,4},{4,5},{5,6},{6,7},{7,8},{8,9},{9,10},{10,1... | collective-permute-start | bytes 393224 | tf_op jit(solution)/shard_map/while/body/eval_jaxpr/ppermute | solution.py:18
  89.7 8.6 %collective-permute-start = (bf16[128,512]{1,0:T(8,128)(2,1)S(1)}, bf16[128,512]{1,0:T(8,128)(2,1)S(1)}, u32[]{:S(2)}, u32[]{:S(2)}) collective-permute-start(bf16[128,512]{1,0:T(8,128)(2,1)S(1)} %get-tuple-element.1222), channel_id=1, source_target_pairs={{0,1},{1,2},{2,3},{3,4},{4,5},{5,6},{6,7},{7,8},{8,9},{9,10},{10,1... | collective-permute-start | bytes 393224 | tf_op jit(solution)/shard_map/while/body/eval_jaxpr/ppermute | solution.py:18
  99.0 9.1 %collective-permute-start = (bf16[128,512]{1,0:T(8,128)(2,1)S(1)}, bf16[128,512]{1,0:T(8,128)(2,1)S(1)}, u32[]{:S(2)}, u32[]{:S(2)}) collective-permute-start(bf16[128,512]{1,0:T(8,128)(2,1)S(1)} %get-tuple-element.1222), channel_id=1, source_target_pairs={{0,1},{1,2},{2,3},{3,4},{4,5},{5,6},{6,7},{7,8},{8,9},{9,10},{10,1... | collective-permute-start | bytes 393224 | tf_op jit(solution)/shard_map/while/body/eval_jaxpr/ppermute | solution.py:18
  108.8 8.6 %collective-permute-start = (bf16[128,512]{1,0:T(8,128)(2,1)S(1)}, bf16[128,512]{1,0:T(8,128)(2,1)S(1)}, u32[]{:S(2)}, u32[]{:S(2)}) collective-permute-start(bf16[128,512]{1,0:T(8,128)(2,1)S(1)} %get-tuple-element.1222), channel_id=1, source_target_pairs={{0,1},{1,2},{2,3},{3,4},{4,5},{5,6},{6,7},{7,8},{8,9},{9,10},{10,1... | collective-permute-start | bytes 393224 | tf_op jit(solution)/shard_map/while/body/eval_jaxpr/ppermute | solution.py:18
  127.1 9.1 %collective-permute-start = (bf16[128,512]{1,0:T(8,128)(2,1)S(1)}, bf16[128,512]{1,0:T(8,128)(2,1)S(1)}, u32[]{:S(2)}, u32[]{:S(2)}) collective-permute-start(bf16[128,512]{1,0:T(8,128)(2,1)S(1)} %get-tuple-element.1222), channel_id=1, source_target_pairs={{0,1},{1,2},{2,3},{3,4},{4,5},{5,6},{6,7},{7,8},{8,9},{9,10},{10,1... | collective-permute-start | bytes 393224 | tf_op jit(solution)/shard_map/while/body/eval_jaxpr/ppermute | solution.py:18
  137.0 9.7 %collective-permute-start = (bf16[128,512]{1,0:T(8,128)(2,1)S(1)}, bf16[128,512]{1,0:T(8,128)(2,1)S(1)}, u32[]{:S(2)}, u32[]{:S(2)}) collective-permute-start(bf16[128,512]{1,0:T(8,128)(2,1)S(1)} %get-tuple-element.1222), channel_id=1, source_target_pairs={{0,1},{1,2},{2,3},{3,4},{4,5},{5,6},{6,7},{7,8},{8,9},{9,10},{10,1... | collective-permute-start | bytes 393224 | tf_op jit(solution)/shard_map/while/body/eval_jaxpr/ppermute | solution.py:18
  231.4 9.1 %collective-permute-start.2 = (f32[128,512]{1,0:T(8,128)S(1)}, f32[128,512]{1,0:T(8,128)S(1)}, u32[]{:S(2)}, u32[]{:S(2)}) collective-permute-start(f32[128,512]{1,0:T(8,128)S(1)} %get-tuple-element.1333), channel_id=1, source_target_pairs={{1,0},{2,1},{3,2},{4,3},{5,4},{6,5},{7,6},{8,7},{9,8},{10,9},{11,1... | collective-permute-start | bytes 786440 | tf_op jit(solution)/shard_map/while/body/eval_jaxpr/ppermute | solution.py:18
  241.5 9.0 %collective-permute-start.2 = (f32[128,512]{1,0:T(8,128)S(1)}, f32[128,512]{1,0:T(8,128)S(1)}, u32[]{:S(2)}, u32[]{:S(2)}) collective-permute-start(f32[128,512]{1,0:T(8,128)S(1)} %get-tuple-element.1333), channel_id=1, source_target_pairs={{1,0},{2,1},{3,2},{4,3},{5,4},{6,5},{7,6},{8,7},{9,8},{10,9},{11,1... | collective-permute-start | bytes 786440 | tf_op jit(solution)/shard_map/while/body/eval_jaxpr/ppermute | solution.py:18
  251.5 11.5 %collective-permute-start.2 = (f32[128,512]{1,0:T(8,128)S(1)}, f32[128,512]{1,0:T(8,128)S(1)}, u32[]{:S(2)}, u32[]{:S(2)}) collective-permute-start(f32[128,512]{1,0:T(8,128)S(1)} %get-tuple-element.1333), channel_id=1, source_target_pairs={{1,0},{2,1},{3,2},{4,3},{5,4},{6,5},{7,6},{8,7},{9,8},{10,9},{11,1... | collective-permute-start | bytes 786440 | tf_op jit(solution)/shard_map/while/body/eval_jaxpr/ppermute | solution.py:18
  264.0 12.7 %collective-permute-start.2 = (f32[128,512]{1,0:T(8,128)S(1)}, f32[128,512]{1,0:T(8,128)S(1)}, u32[]{:S(2)}, u32[]{:S(2)}) collective-permute-start(f32[128,512]{1,0:T(8,128)S(1)} %get-tuple-element.1333), channel_id=1, source_target_pairs={{1,0},{2,1},{3,2},{4,3},{5,4},{6,5},{7,6},{8,7},{9,8},{10,9},{11,1... | collective-permute-start | bytes 786440 | tf_op jit(solution)/shard_map/while/body/eval_jaxpr/ppermute | solution.py:18
  277.7 10.5 %collective-permute-start.2 = (f32[128,512]{1,0:T(8,128)S(1)}, f32[128,512]{1,0:T(8,128)S(1)}, u32[]{:S(2)}, u32[]{:S(2)}) collective-permute-start(f32[128,512]{1,0:T(8,128)S(1)} %get-tuple-element.1333), channel_id=1, source_target_pairs={{1,0},{2,1},{3,2},{4,3},{5,4},{6,5},{7,6},{8,7},{9,8},{10,9},{11,1... | collective-permute-start | bytes 786440 | tf_op jit(solution)/shard_map/while/body/eval_jaxpr/ppermute | solution.py:18
  289.2 8.7 %collective-permute-start.2 = (f32[128,512]{1,0:T(8,128)S(1)}, f32[128,512]{1,0:T(8,128)S(1)}, u32[]{:S(2)}, u32[]{:S(2)}) collective-permute-start(f32[128,512]{1,0:T(8,128)S(1)} %get-tuple-element.1333), channel_id=1, source_target_pairs={{1,0},{2,1},{3,2},{4,3},{5,4},{6,5},{7,6},{8,7},{9,8},{10,9},{11,1... | collective-permute-start | bytes 786440 | tf_op jit(solution)/shard_map/while/body/eval_jaxpr/ppermute | solution.py:18
  308.0 8.9 %collective-permute-start.2 = (f32[128,512]{1,0:T(8,128)S(1)}, f32[128,512]{1,0:T(8,128)S(1)}, u32[]{:S(2)}, u32[]{:S(2)}) collective-permute-start(f32[128,512]{1,0:T(8,128)S(1)} %get-tuple-element.1333), channel_id=1, source_target_pairs={{1,0},{2,1},{3,2},{4,3},{5,4},{6,5},{7,6},{8,7},{9,8},{10,9},{11,1... | collective-permute-start | bytes 786440 | tf_op jit(solution)/shard_map/while/body/eval_jaxpr/ppermute | solution.py:18
  317.9 9.2 %collective-permute-start.2 = (f32[128,512]{1,0:T(8,128)S(1)}, f32[128,512]{1,0:T(8,128)S(1)}, u32[]{:S(2)}, u32[]{:S(2)}) collective-permute-start(f32[128,512]{1,0:T(8,128)S(1)} %get-tuple-element.1333), channel_id=1, source_target_pairs={{1,0},{2,1},{3,2},{4,3},{5,4},{6,5},{7,6},{8,7},{9,8},{10,9},{11,1... | collective-permute-start | bytes 786440 | tf_op jit(solution)/shard_map/while/body/eval_jaxpr/ppermute | solution.py:18
  328.1 9.2 %collective-permute-start.2 = (f32[128,512]{1,0:T(8,128)S(1)}, f32[128,512]{1,0:T(8,128)S(1)}, u32[]{:S(2)}, u32[]{:S(2)}) collective-permute-start(f32[128,512]{1,0:T(8,128)S(1)} %get-tuple-element.1333), channel_id=1, source_target_pairs={{1,0},{2,1},{3,2},{4,3},{5,4},{6,5},{7,6},{8,7},{9,8},{10,9},{11,1... | collective-permute-start | bytes 786440 | tf_op jit(solution)/shard_map/while/body/eval_jaxpr/ppermute | solution.py:18
  338.4 9.2 %collective-permute-start.2 = (f32[128,512]{1,0:T(8,128)S(1)}, f32[128,512]{1,0:T(8,128)S(1)}, u32[]{:S(2)}, u32[]{:S(2)}) collective-permute-start(f32[128,512]{1,0:T(8,128)S(1)} %get-tuple-element.1333), channel_id=1, source_target_pairs={{1,0},{2,1},{3,2},{4,3},{5,4},{6,5},{7,6},{8,7},{9,8},{10,9},{11,1... | collective-permute-start | bytes 786440 | tf_op jit(solution)/shard_map/while/body/eval_jaxpr/ppermute | solution.py:18
  348.6 10.1 %collective-permute-start.2 = (f32[128,512]{1,0:T(8,128)S(1)}, f32[128,512]{1,0:T(8,128)S(1)}, u32[]{:S(2)}, u32[]{:S(2)}) collective-permute-start(f32[128,512]{1,0:T(8,128)S(1)} %get-tuple-element.1333), channel_id=1, source_target_pairs={{1,0},{2,1},{3,2},{4,3},{5,4},{6,5},{7,6},{8,7},{9,8},{10,9},{11,1... | collective-permute-start | bytes 786440 | tf_op jit(solution)/shard_map/while/body/eval_jaxpr/ppermute | solution.py:18
  359.7 11.7 %collective-permute-start.2 = (f32[128,512]{1,0:T(8,128)S(1)}, f32[128,512]{1,0:T(8,128)S(1)}, u32[]{:S(2)}, u32[]{:S(2)}) collective-permute-start(f32[128,512]{1,0:T(8,128)S(1)} %get-tuple-element.1333), channel_id=1, source_target_pairs={{1,0},{2,1},{3,2},{4,3},{5,4},{6,5},{7,6},{8,7},{9,8},{10,9},{11,1... | collective-permute-start | bytes 786440 | tf_op jit(solution)/shard_map/while/body/eval_jaxpr/ppermute | solution.py:18
  372.4 12.8 %collective-permute-start.2 = (f32[128,512]{1,0:T(8,128)S(1)}, f32[128,512]{1,0:T(8,128)S(1)}, u32[]{:S(2)}, u32[]{:S(2)}) collective-permute-start(f32[128,512]{1,0:T(8,128)S(1)} %get-tuple-element.1333), channel_id=1, source_target_pairs={{1,0},{2,1},{3,2},{4,3},{5,4},{6,5},{7,6},{8,7},{9,8},{10,9},{11,1... | collective-permute-start | bytes 786440 | tf_op jit(solution)/shard_map/while/body/eval_jaxpr/ppermute | solution.py:18
  (23 other events, 263.3 us)
where the time goes:
time: 567 us; the launch traced here: 564 us
  blocking collectives  175 us (31%)
  waiting for transfers between devices  139 us (25%)
  starting transfers between devices  136 us (24%)
  local copies, waits for them, and re-layouts  47.1 us (8%)
  matrix products  34.2 us (6%)
  other arithmetic  24 us (4%)
  loops' own time  6.87 us (1%)
    psum x1, blocking collectives, local(): grad_bias = lax.psum(jnp.sum(query_grad, axis=0), ('dp', 'ctx'))  175 us
    ppermute x45, waiting for transfers between devices, passed_along(): lax.ppermute(value, axis, [(source, source + steps) for source in range(f...  139 us
    ppermute x45, starting transfers between devices, passed_along(): lax.ppermute(value, axis, [(source, source + steps) for source in range(f...  136 us
    add x15, other arithmetic, return_partial(): returned + lax.dynamic_index_in_dim(partials, window_slots - 1 - step_ind...  14.8 us
  transfers between devices with their start and end apart: 45, of which 30 were waited for; matrix products, arithmetic and copies ran while one was open for 0% of the time, Pallas kernels for 0%

commit v1 on v0

--- a/solution.py
+++ b/solution.py
@@ -184,7 +184,7 @@
     summed_total = lax.fori_loop(1, window_slots, return_partial, partials[window_slots - 1])
     key_gradient = summed_total[:, : KEY_VALUE_HEADS * HEAD_SIZE].astype(jnp.bfloat16)
     value_gradient = summed_total[:, KEY_VALUE_HEADS * HEAD_SIZE :].astype(jnp.bfloat16)
-    grad_bias = lax.psum(jnp.sum(query_grad, axis=0), ("dp", "ctx"))
+    grad_bias = lax.psum(lax.psum(jnp.sum(query_grad, axis=0), "ctx"), "dp")
     attended_out = attended.reshape(sharded_rows, QUERY_HEADS * HEAD_SIZE)
     return (
         attended_out[None],

time: 567 us -> 615 us (1.085)
  the two profiles are of different devices: /device:TPU:1 before, /device:TPU:385 now
where the time goes in v1:
time: 615 us; the launch traced here: 612 us
  blocking collectives  192 us (31%)
  starting transfers between devices  164 us (27%)
  waiting for transfers between devices  143 us (23%)
  local copies, waits for them, and re-layouts  47 us (8%)
  matrix products  34.2 us (6%)
  other arithmetic  23.9 us (4%)
  loops' own time  6.91 us (1%)
    psum x2, blocking collectives, local(): grad_bias = lax.psum(lax.psum(jnp.sum(query_grad, axis=0), 'ctx'), 'dp')  192 us
    ppermute x45, starting transfers between devices, passed_along(): lax.ppermute(value, axis, [(source, source + steps) for source in range(f...  164 us
    ppermute x45, waiting for transfers between devices, passed_along(): lax.ppermute(value, axis, [(source, source + steps) for source in range(f...  143 us
    add x15, other arithmetic, return_partial(): returned + lax.dynamic_index_in_dim(partials, window_slots - 1 - step_ind...  14.8 us
  transfers between devices with their start and end apart: 45, of which 30 were waited for; matrix products, arithmetic and copies ran while one was open for 0% of the time, Pallas kernels for 0%

profile of v1, /device:TPU:385, one launch (start us, length us, event | category | flops | bytes accessed | tf_op | source)
XLA Modules:
  0.0 612.3 jit_solution(14547718030963852340)
XLA Ops:
  8.9 156.2 %while.72 = (s32[]{:T(128)}, bf16[16,128,512]{2,1,0:T(8,128)(2,1)}, s32[16,128]{1,0:T(8,128)S(1)}, bf16[128,512]{1,0:T(8,128)(2,1)S(1)}, s32[128]{0:T(128)S(1)}, /*index=5*/s32[]{:T(128)}, s32[]{:T(128)}, s32[]{:T(128)}) while((s32[]{:T(128)}, bf16[16,128,512]{2,1,0:T(8,128)(2,1)}, s32[16,128]{1,0:T(8,128)S(1)}, ...), condition=%wide.region_1.2_spmd, body=%wide.region_0.1_spmd.sunk | while | flops 5 | bytes 1052879 | solution.py:67
  96.0 5.9 collective-permute-done.1
  106.4 6.5 %collective-permute-done.1 = s32[128]{0:T(128)S(1)} collective-permute-done((s32[128]{0:T(128)S(1)}, s32[128]{0:T(128)S(1)}, u32[]{:S(2)}, u32[]{:S(2)}) %collective-permute-start.1) | collective-permute-done | bytes 544 | tf_op jit(solution)/shard_map/while/body/eval_jaxpr/ppermute | solution.py:18
  117.5 6.0 collective-permute-done.1
  169.3 23.1 %while.74 = (s32[]{:T(128)}, f32[2,7,128]{2,1,0:T(8,128)S(1)}, f32[2,7,128]{2,1,0:T(8,128)S(1)}, f32[2,7,128,128]{3,2,1,0:T(8,128)S(1)}, s32[4]{0:T(128)S(1)}, /...) while((s32[]{:T(128)}, f32[2,7,128]{2,1,0:T(8,128)S(1)}, ...), condition=%wide.region_5.6_spmd.clone.clone.clone, body=%wide.region_2.5_spmd.clone.clone.clone.sunk | while | flops 480120704 | bytes 16320205 | solution.py:125
  197.1 42.8 %while.75 = (s32[]{:T(128)}, f32[128,2,7,128]{0,3,2,1:T(8,128)S(1)}, f32[4,512,512]{2,1,0:T(8,128)}, bf16[4,512,512]{1,2,0:T(8,128)(2,1)}, s32[4]{0:T(128)S(1)},...) while((s32[]{:T(128)}, ...), condition=%wide.region_7.8_spmd.clone.clone.clone, body=%wide.region_6.7_spmd.clone.clone.clone.sunk | while | flops 1184918656 | bytes 30644960 | solution.py:170
  240.8 177.1 %while.73 = (s32[]{:T(128)}, f32[128,512]{1,0:T(8,128)S(1)}, f32[16,128,512]{2,1,0:T(8,128)}, s32[]{:T(128)}, s32[]{:T(128)}, /*index=5*/s32[]{:T(128)}, s32[]{:T(128)}) while((s32[]{:T(128)}, f32[128,512]{1,0:T(8,128)S(1)}, f32[16,128,512]{2,1,0:T(8,128)}, s32[]{:T(128)}, s32[]{:T(128)}, /*index=5*/s32[]{:T(128)}, s32[]{:T(128)}) %tuple.177), condition=%wide.region_9.10_spmd, body=%wide.region_8.9_spmd.sunk | while | flops 65542 | bytes 1835175 | solution.py:184
  248.9 6.7 %collective-permute-start.2 = (f32[128,512]{1,0:T(8,128)S(1)}, f32[128,512]{1,0:T(8,128)S(1)}, u32[]{:S(2)}, u32[]{:S(2)}) collective-permute-start(f32[128,512]{1,0:T(8,128)S(1)} %get-tuple-element.1333), channel_id=1, source_target_pairs={{1,0},{2,1},{3,2},{4,3},{5,4},{6,5},{7,6},{8,7},{9,8},{10,9},{11,1... | collective-permute-start | bytes 786440 | tf_op jit(solution)/shard_map/while/body/eval_jaxpr/ppermute | solution.py:18
  260.0 7.1 %collective-permute-start.2 = (f32[128,512]{1,0:T(8,128)S(1)}, f32[128,512]{1,0:T(8,128)S(1)}, u32[]{:S(2)}, u32[]{:S(2)}) collective-permute-start(f32[128,512]{1,0:T(8,128)S(1)} %get-tuple-element.1333), channel_id=1, source_target_pairs={{1,0},{2,1},{3,2},{4,3},{5,4},{6,5},{7,6},{8,7},{9,8},{10,9},{11,1... | collective-permute-start | bytes 786440 | tf_op jit(solution)/shard_map/while/body/eval_jaxpr/ppermute | solution.py:18
  271.4 7.1 %collective-permute-start.2 = (f32[128,512]{1,0:T(8,128)S(1)}, f32[128,512]{1,0:T(8,128)S(1)}, u32[]{:S(2)}, u32[]{:S(2)}) collective-permute-start(f32[128,512]{1,0:T(8,128)S(1)} %get-tuple-element.1333), channel_id=1, source_target_pairs={{1,0},{2,1},{3,2},{4,3},{5,4},{6,5},{7,6},{8,7},{9,8},{10,9},{11,1... | collective-permute-start | bytes 786440 | tf_op jit(solution)/shard_map/while/body/eval_jaxpr/ppermute | solution.py:18
  282.8 7.1 %collective-permute-start.2 = (f32[128,512]{1,0:T(8,128)S(1)}, f32[128,512]{1,0:T(8,128)S(1)}, u32[]{:S(2)}, u32[]{:S(2)}) collective-permute-start(f32[128,512]{1,0:T(8,128)S(1)} %get-tuple-element.1333), channel_id=1, source_target_pairs={{1,0},{2,1},{3,2},{4,3},{5,4},{6,5},{7,6},{8,7},{9,8},{10,9},{11,1... | collective-permute-start | bytes 786440 | tf_op jit(solution)/shard_map/while/body/eval_jaxpr/ppermute | solution.py:18
  294.8 7.1 %collective-permute-start.2 = (f32[128,512]{1,0:T(8,128)S(1)}, f32[128,512]{1,0:T(8,128)S(1)}, u32[]{:S(2)}, u32[]{:S(2)}) collective-permute-start(f32[128,512]{1,0:T(8,128)S(1)} %get-tuple-element.1333), channel_id=1, source_target_pairs={{1,0},{2,1},{3,2},{4,3},{5,4},{6,5},{7,6},{8,7},{9,8},{10,9},{11,1... | collective-permute-start | bytes 786440 | tf_op jit(solution)/shard_map/while/body/eval_jaxpr/ppermute | solution.py:18
  307.9 7.1 %collective-permute-start.2 = (f32[128,512]{1,0:T(8,128)S(1)}, f32[128,512]{1,0:T(8,128)S(1)}, u32[]{:S(2)}, u32[]{:S(2)}) collective-permute-start(f32[128,512]{1,0:T(8,128)S(1)} %get-tuple-element.1333), channel_id=1, source_target_pairs={{1,0},{2,1},{3,2},{4,3},{5,4},{6,5},{7,6},{8,7},{9,8},{10,9},{11,1... | collective-permute-start | bytes 786440 | tf_op jit(solution)/shard_map/while/body/eval_jaxpr/ppermute | solution.py:18
  315.1 6.1 collective-permute-done.2
  322.2 7.3 %collective-permute-start.2 = (f32[128,512]{1,0:T(8,128)S(1)}, f32[128,512]{1,0:T(8,128)S(1)}, u32[]{:S(2)}, u32[]{:S(2)}) collective-permute-start(f32[128,512]{1,0:T(8,128)S(1)} %get-tuple-element.1333), channel_id=1, source_target_pairs={{1,0},{2,1},{3,2},{4,3},{5,4},{6,5},{7,6},{8,7},{9,8},{10,9},{11,1... | collective-permute-start | bytes 786440 | tf_op jit(solution)/shard_map/while/body/eval_jaxpr/ppermute | solution.py:18
  335.8 7.4 %collective-permute-start.2 = (f32[128,512]{1,0:T(8,128)S(1)}, f32[128,512]{1,0:T(8,128)S(1)}, u32[]{:S(2)}, u32[]{:S(2)}) collective-permute-start(f32[128,512]{1,0:T(8,128)S(1)} %get-tuple-element.1333), channel_id=1, source_target_pairs={{1,0},{2,1},{3,2},{4,3},{5,4},{6,5},{7,6},{8,7},{9,8},{10,9},{11,1... | collective-permute-start | bytes 786440 | tf_op jit(solution)/shard_map/while/body/eval_jaxpr/ppermute | solution.py:18
  348.6 7.4 %collective-permute-start.2 = (f32[128,512]{1,0:T(8,128)S(1)}, f32[128,512]{1,0:T(8,128)S(1)}, u32[]{:S(2)}, u32[]{:S(2)}) collective-permute-start(f32[128,512]{1,0:T(8,128)S(1)} %get-tuple-element.1333), channel_id=1, source_target_pairs={{1,0},{2,1},{3,2},{4,3},{5,4},{6,5},{7,6},{8,7},{9,8},{10,9},{11,1... | collective-permute-start | bytes 786440 | tf_op jit(solution)/shard_map/while/body/eval_jaxpr/ppermute | solution.py:18
  360.3 7.6 %collective-permute-start.2 = (f32[128,512]{1,0:T(8,128)S(1)}, f32[128,512]{1,0:T(8,128)S(1)}, u32[]{:S(2)}, u32[]{:S(2)}) collective-permute-start(f32[128,512]{1,0:T(8,128)S(1)} %get-tuple-element.1333), channel_id=1, source_target_pairs={{1,0},{2,1},{3,2},{4,3},{5,4},{6,5},{7,6},{8,7},{9,8},{10,9},{11,1... | collective-permute-start | bytes 786440 | tf_op jit(solution)/shard_map/while/body/eval_jaxpr/ppermute | solution.py:18
  372.2 7.1 %collective-permute-start.2 = (f32[128,512]{1,0:T(8,128)S(1)}, f32[128,512]{1,0:T(8,128)S(1)}, u32[]{:S(2)}, u32[]{:S(2)}) collective-permute-start(f32[128,512]{1,0:T(8,128)S(1)} %get-tuple-element.1333), channel_id=1, source_target_pairs={{1,0},{2,1},{3,2},{4,3},{5,4},{6,5},{7,6},{8,7},{9,8},{10,9},{11,1... | collective-permute-start | bytes 786440 | tf_op jit(solution)/shard_map/while/body/eval_jaxpr/ppermute | solution.py:18
  383.6 7.1 %collective-permute-start.2 = (f32[128,512]{1,0:T(8,128)S(1)}, f32[128,512]{1,0:T(8,128)S(1)}, u32[]{:S(2)}, u32[]{:S(2)}) collective-permute-start(f32[128,512]{1,0:T(8,128)S(1)} %get-tuple-element.1333), channel_id=1, source_target_pairs={{1,0},{2,1},{3,2},{4,3},{5,4},{6,5},{7,6},{8,7},{9,8},{10,9},{11,1... | collective-permute-start | bytes 786440 | tf_op jit(solution)/shard_map/while/body/eval_jaxpr/ppermute | solution.py:18
  395.0 7.1 %collective-permute-start.2 = (f32[128,512]{1,0:T(8,128)S(1)}, f32[128,512]{1,0:T(8,128)S(1)}, u32[]{:S(2)}, u32[]{:S(2)}) collective-permute-start(f32[128,512]{1,0:T(8,128)S(1)} %get-tuple-element.1333), channel_id=1, source_target_pairs={{1,0},{2,1},{3,2},{4,3},{5,4},{6,5},{7,6},{8,7},{9,8},{10,9},{11,1... | collective-permute-start | bytes 786440 | tf_op jit(solution)/shard_map/while/body/eval_jaxpr/ppermute | solution.py:18
  406.5 7.1 %collective-permute-start.2 = (f32[128,512]{1,0:T(8,128)S(1)}, f32[128,512]{1,0:T(8,128)S(1)}, u32[]{:S(2)}, u32[]{:S(2)}) collective-permute-start(f32[128,512]{1,0:T(8,128)S(1)} %get-tuple-element.1333), channel_id=1, source_target_pairs={{1,0},{2,1},{3,2},{4,3},{5,4},{6,5},{7,6},{8,7},{9,8},{10,9},{11,1... | collective-permute-start | bytes 786440 | tf_op jit(solution)/shard_map/while/body/eval_jaxpr/ppermute | solution.py:18
  418.9 117.4 %psum.14 = f32[1792]{0:T(1024)S(1)} all-reduce(f32[1792]{0:T(1024)S(1)} %reduce_sum.25), channel_id=1, replica_groups=mesh['dp'=8,'ctx'=64] {'ctx'}, use_global_device_ids=true, to_apply=%region_11.12 | all-reduce | flops 1792 | bytes 14336 | tf_op jit(solution)/shard_map/psum | solution.py:187
  536.3 74.9 %psum.15 = f32[1792]{0:T(1024)} all-reduce(f32[1792]{0:T(1024)S(1)} %psum.14), channel_id=1, replica_groups=mesh['dp'=8,'ctx'=64] {'dp'}, use_global_device_ids=true, to_apply=%region_12.13 | all-reduce | flops 1792 | bytes 14336 | tf_op jit(solution)/shard_map/psum | solution.py:187
  (299 shorter events, 287.1 us)
Async XLA Ops:
  8.9 10.9 %collective-permute-start = (bf16[128,512]{1,0:T(8,128)(2,1)S(1)}, bf16[128,512]{1,0:T(8,128)(2,1)S(1)}, u32[]{:S(2)}, u32[]{:S(2)}) collective-permute-start(bf16[128,512]{1,0:T(8,128)(2,1)S(1)} %get-tuple-element.1222), channel_id=1, source_target_pairs={{0,1},{1,2},{2,3},{3,4},{4,5},{5,6},{6,7},{7,8},{8,9},{9,10},{10,1... | collective-permute-start | bytes 393224 | tf_op jit(solution)/shard_map/while/body/eval_jaxpr/ppermute | solution.py:18
  20.5 9.6 %collective-permute-start = (bf16[128,512]{1,0:T(8,128)(2,1)S(1)}, bf16[128,512]{1,0:T(8,128)(2,1)S(1)}, u32[]{:S(2)}, u32[]{:S(2)}) collective-permute-start(bf16[128,512]{1,0:T(8,128)(2,1)S(1)} %get-tuple-element.1222), channel_id=1, source_target_pairs={{0,1},{1,2},{2,3},{3,4},{4,5},{5,6},{6,7},{7,8},{8,9},{9,10},{10,1... | collective-permute-start | bytes 393224 | tf_op jit(solution)/shard_map/while/body/eval_jaxpr/ppermute | solution.py:18
  30.7 9.6 %collective-permute-start = (bf16[128,512]{1,0:T(8,128)(2,1)S(1)}, bf16[128,512]{1,0:T(8,128)(2,1)S(1)}, u32[]{:S(2)}, u32[]{:S(2)}) collective-permute-start(bf16[128,512]{1,0:T(8,128)(2,1)S(1)} %get-tuple-element.1222), channel_id=1, source_target_pairs={{0,1},{1,2},{2,3},{3,4},{4,5},{5,6},{6,7},{7,8},{8,9},{9,10},{10,1... | collective-permute-start | bytes 393224 | tf_op jit(solution)/shard_map/while/body/eval_jaxpr/ppermute | solution.py:18
  40.9 9.6 %collective-permute-start = (bf16[128,512]{1,0:T(8,128)(2,1)S(1)}, bf16[128,512]{1,0:T(8,128)(2,1)S(1)}, u32[]{:S(2)}, u32[]{:S(2)}) collective-permute-start(bf16[128,512]{1,0:T(8,128)(2,1)S(1)} %get-tuple-element.1222), channel_id=1, source_target_pairs={{0,1},{1,2},{2,3},{3,4},{4,5},{5,6},{6,7},{7,8},{8,9},{9,10},{10,1... | collective-permute-start | bytes 393224 | tf_op jit(solution)/shard_map/while/body/eval_jaxpr/ppermute | solution.py:18
  51.2 9.6 %collective-permute-start = (bf16[128,512]{1,0:T(8,128)(2,1)S(1)}, bf16[128,512]{1,0:T(8,128)(2,1)S(1)}, u32[]{:S(2)}, u32[]{:S(2)}) collective-permute-start(bf16[128,512]{1,0:T(8,128)(2,1)S(1)} %get-tuple-element.1222), channel_id=1, source_target_pairs={{0,1},{1,2},{2,3},{3,4},{4,5},{5,6},{6,7},{7,8},{8,9},{9,10},{10,1... | collective-permute-start | bytes 393224 | tf_op jit(solution)/shard_map/while/body/eval_jaxpr/ppermute | solution.py:18
  92.1 9.7 %collective-permute-start = (bf16[128,512]{1,0:T(8,128)(2,1)S(1)}, bf16[128,512]{1,0:T(8,128)(2,1)S(1)}, u32[]{:S(2)}, u32[]{:S(2)}) collective-permute-start(bf16[128,512]{1,0:T(8,128)(2,1)S(1)} %get-tuple-element.1222), channel_id=1, source_target_pairs={{0,1},{1,2},{2,3},{3,4},{4,5},{5,6},{6,7},{7,8},{8,9},{9,10},{10,1... | collective-permute-start | bytes 393224 | tf_op jit(solution)/shard_map/while/body/eval_jaxpr/ppermute | solution.py:18
  102.5 10.4 %collective-permute-start = (bf16[128,512]{1,0:T(8,128)(2,1)S(1)}, bf16[128,512]{1,0:T(8,128)(2,1)S(1)}, u32[]{:S(2)}, u32[]{:S(2)}) collective-permute-start(bf16[128,512]{1,0:T(8,128)(2,1)S(1)} %get-tuple-element.1222), channel_id=1, source_target_pairs={{0,1},{1,2},{2,3},{3,4},{4,5},{5,6},{6,7},{7,8},{8,9},{9,10},{10,1... | collective-permute-start | bytes 393224 | tf_op jit(solution)/shard_map/while/body/eval_jaxpr/ppermute | solution.py:18
  113.6 9.8 %collective-permute-start = (bf16[128,512]{1,0:T(8,128)(2,1)S(1)}, bf16[128,512]{1,0:T(8,128)(2,1)S(1)}, u32[]{:S(2)}, u32[]{:S(2)}) collective-permute-start(bf16[128,512]{1,0:T(8,128)(2,1)S(1)} %get-tuple-element.1222), channel_id=1, source_target_pairs={{0,1},{1,2},{2,3},{3,4},{4,5},{5,6},{6,7},{7,8},{8,9},{9,10},{10,1... | collective-permute-start | bytes 393224 | tf_op jit(solution)/shard_map/while/body/eval_jaxpr/ppermute | solution.py:18
  124.2 9.6 %collective-permute-start = (bf16[128,512]{1,0:T(8,128)(2,1)S(1)}, bf16[128,512]{1,0:T(8,128)(2,1)S(1)}, u32[]{:S(2)}, u32[]{:S(2)}) collective-permute-start(bf16[128,512]{1,0:T(8,128)(2,1)S(1)} %get-tuple-element.1222), channel_id=1, source_target_pairs={{0,1},{1,2},{2,3},{3,4},{4,5},{5,6},{6,7},{7,8},{8,9},{9,10},{10,1... | collective-permute-start | bytes 393224 | tf_op jit(solution)/shard_map/while/body/eval_jaxpr/ppermute | solution.py:18
  134.4 9.6 %collective-permute-start = (bf16[128,512]{1,0:T(8,128)(2,1)S(1)}, bf16[128,512]{1,0:T(8,128)(2,1)S(1)}, u32[]{:S(2)}, u32[]{:S(2)}) collective-permute-start(bf16[128,512]{1,0:T(8,128)(2,1)S(1)} %get-tuple-element.1222), channel_id=1, source_target_pairs={{0,1},{1,2},{2,3},{3,4},{4,5},{5,6},{6,7},{7,8},{8,9},{9,10},{10,1... | collective-permute-start | bytes 393224 | tf_op jit(solution)/shard_map/while/body/eval_jaxpr/ppermute | solution.py:18
  248.9 10.0 %collective-permute-start.2 = (f32[128,512]{1,0:T(8,128)S(1)}, f32[128,512]{1,0:T(8,128)S(1)}, u32[]{:S(2)}, u32[]{:S(2)}) collective-permute-start(f32[128,512]{1,0:T(8,128)S(1)} %get-tuple-element.1333), channel_id=1, source_target_pairs={{1,0},{2,1},{3,2},{4,3},{5,4},{6,5},{7,6},{8,7},{9,8},{10,9},{11,1... | collective-permute-start | bytes 786440 | tf_op jit(solution)/shard_map/while/body/eval_jaxpr/ppermute | solution.py:18
  260.0 10.4 %collective-permute-start.2 = (f32[128,512]{1,0:T(8,128)S(1)}, f32[128,512]{1,0:T(8,128)S(1)}, u32[]{:S(2)}, u32[]{:S(2)}) collective-permute-start(f32[128,512]{1,0:T(8,128)S(1)} %get-tuple-element.1333), channel_id=1, source_target_pairs={{1,0},{2,1},{3,2},{4,3},{5,4},{6,5},{7,6},{8,7},{9,8},{10,9},{11,1... | collective-permute-start | bytes 786440 | tf_op jit(solution)/shard_map/while/body/eval_jaxpr/ppermute | solution.py:18
  271.4 10.4 %collective-permute-start.2 = (f32[128,512]{1,0:T(8,128)S(1)}, f32[128,512]{1,0:T(8,128)S(1)}, u32[]{:S(2)}, u32[]{:S(2)}) collective-permute-start(f32[128,512]{1,0:T(8,128)S(1)} %get-tuple-element.1333), channel_id=1, source_target_pairs={{1,0},{2,1},{3,2},{4,3},{5,4},{6,5},{7,6},{8,7},{9,8},{10,9},{11,1... | collective-permute-start | bytes 786440 | tf_op jit(solution)/shard_map/while/body/eval_jaxpr/ppermute | solution.py:18
  282.8 11.0 %collective-permute-start.2 = (f32[128,512]{1,0:T(8,128)S(1)}, f32[128,512]{1,0:T(8,128)S(1)}, u32[]{:S(2)}, u32[]{:S(2)}) collective-permute-start(f32[128,512]{1,0:T(8,128)S(1)} %get-tuple-element.1333), channel_id=1, source_target_pairs={{1,0},{2,1},{3,2},{4,3},{5,4},{6,5},{7,6},{8,7},{9,8},{10,9},{11,1... | collective-permute-start | bytes 786440 | tf_op jit(solution)/shard_map/while/body/eval_jaxpr/ppermute | solution.py:18
  294.8 12.1 %collective-permute-start.2 = (f32[128,512]{1,0:T(8,128)S(1)}, f32[128,512]{1,0:T(8,128)S(1)}, u32[]{:S(2)}, u32[]{:S(2)}) collective-permute-start(f32[128,512]{1,0:T(8,128)S(1)} %get-tuple-element.1333), channel_id=1, source_target_pairs={{1,0},{2,1},{3,2},{4,3},{5,4},{6,5},{7,6},{8,7},{9,8},{10,9},{11,1... | collective-permute-start | bytes 786440 | tf_op jit(solution)/shard_map/while/body/eval_jaxpr/ppermute | solution.py:18
  307.9 13.2 %collective-permute-start.2 = (f32[128,512]{1,0:T(8,128)S(1)}, f32[128,512]{1,0:T(8,128)S(1)}, u32[]{:S(2)}, u32[]{:S(2)}) collective-permute-start(f32[128,512]{1,0:T(8,128)S(1)} %get-tuple-element.1333), channel_id=1, source_target_pairs={{1,0},{2,1},{3,2},{4,3},{5,4},{6,5},{7,6},{8,7},{9,8},{10,9},{11,1... | collective-permute-start | bytes 786440 | tf_op jit(solution)/shard_map/while/body/eval_jaxpr/ppermute | solution.py:18
  322.2 12.6 %collective-permute-start.2 = (f32[128,512]{1,0:T(8,128)S(1)}, f32[128,512]{1,0:T(8,128)S(1)}, u32[]{:S(2)}, u32[]{:S(2)}) collective-permute-start(f32[128,512]{1,0:T(8,128)S(1)} %get-tuple-element.1333), channel_id=1, source_target_pairs={{1,0},{2,1},{3,2},{4,3},{5,4},{6,5},{7,6},{8,7},{9,8},{10,9},{11,1... | collective-permute-start | bytes 786440 | tf_op jit(solution)/shard_map/while/body/eval_jaxpr/ppermute | solution.py:18
  335.8 11.8 %collective-permute-start.2 = (f32[128,512]{1,0:T(8,128)S(1)}, f32[128,512]{1,0:T(8,128)S(1)}, u32[]{:S(2)}, u32[]{:S(2)}) collective-permute-start(f32[128,512]{1,0:T(8,128)S(1)} %get-tuple-element.1333), channel_id=1, source_target_pairs={{1,0},{2,1},{3,2},{4,3},{5,4},{6,5},{7,6},{8,7},{9,8},{10,9},{11,1... | collective-permute-start | bytes 786440 | tf_op jit(solution)/shard_map/while/body/eval_jaxpr/ppermute | solution.py:18
  348.6 10.7 %collective-permute-start.2 = (f32[128,512]{1,0:T(8,128)S(1)}, f32[128,512]{1,0:T(8,128)S(1)}, u32[]{:S(2)}, u32[]{:S(2)}) collective-permute-start(f32[128,512]{1,0:T(8,128)S(1)} %get-tuple-element.1333), channel_id=1, source_target_pairs={{1,0},{2,1},{3,2},{4,3},{5,4},{6,5},{7,6},{8,7},{9,8},{10,9},{11,1... | collective-permute-start | bytes 786440 | tf_op jit(solution)/shard_map/while/body/eval_jaxpr/ppermute | solution.py:18
  360.3 10.9 %collective-permute-start.2 = (f32[128,512]{1,0:T(8,128)S(1)}, f32[128,512]{1,0:T(8,128)S(1)}, u32[]{:S(2)}, u32[]{:S(2)}) collective-permute-start(f32[128,512]{1,0:T(8,128)S(1)} %get-tuple-element.1333), channel_id=1, source_target_pairs={{1,0},{2,1},{3,2},{4,3},{5,4},{6,5},{7,6},{8,7},{9,8},{10,9},{11,1... | collective-permute-start | bytes 786440 | tf_op jit(solution)/shard_map/while/body/eval_jaxpr/ppermute | solution.py:18
  372.2 10.4 %collective-permute-start.2 = (f32[128,512]{1,0:T(8,128)S(1)}, f32[128,512]{1,0:T(8,128)S(1)}, u32[]{:S(2)}, u32[]{:S(2)}) collective-permute-start(f32[128,512]{1,0:T(8,128)S(1)} %get-tuple-element.1333), channel_id=1, source_target_pairs={{1,0},{2,1},{3,2},{4,3},{5,4},{6,5},{7,6},{8,7},{9,8},{10,9},{11,1... | collective-permute-start | bytes 786440 | tf_op jit(solution)/shard_map/while/body/eval_jaxpr/ppermute | solution.py:18
  383.6 10.4 %collective-permute-start.2 = (f32[128,512]{1,0:T(8,128)S(1)}, f32[128,512]{1,0:T(8,128)S(1)}, u32[]{:S(2)}, u32[]{:S(2)}) collective-permute-start(f32[128,512]{1,0:T(8,128)S(1)} %get-tuple-element.1333), channel_id=1, source_target_pairs={{1,0},{2,1},{3,2},{4,3},{5,4},{6,5},{7,6},{8,7},{9,8},{10,9},{11,1... | collective-permute-start | bytes 786440 | tf_op jit(solution)/shard_map/while/body/eval_jaxpr/ppermute | solution.py:18
  395.0 10.4 %collective-permute-start.2 = (f32[128,512]{1,0:T(8,128)S(1)}, f32[128,512]{1,0:T(8,128)S(1)}, u32[]{:S(2)}, u32[]{:S(2)}) collective-permute-start(f32[128,512]{1,0:T(8,128)S(1)} %get-tuple-element.1333), channel_id=1, source_target_pairs={{1,0},{2,1},{3,2},{4,3},{5,4},{6,5},{7,6},{8,7},{9,8},{10,9},{11,1... | collective-permute-start | bytes 786440 | tf_op jit(solution)/shard_map/while/body/eval_jaxpr/ppermute | solution.py:18
  406.5 10.4 %collective-permute-start.2 = (f32[128,512]{1,0:T(8,128)S(1)}, f32[128,512]{1,0:T(8,128)S(1)}, u32[]{:S(2)}, u32[]{:S(2)}) collective-permute-start(f32[128,512]{1,0:T(8,128)S(1)} %get-tuple-element.1333), channel_id=1, source_target_pairs={{1,0},{2,1},{3,2},{4,3},{5,4},{6,5},{7,6},{8,7},{9,8},{10,9},{11,1... | collective-permute-start | bytes 786440 | tf_op jit(solution)/shard_map/while/body/eval_jaxpr/ppermute | solution.py:18
  (23 other events, 331.6 us)
